TPU v7x, 256 devices: a whole 4x4x8 slice. The times are simulated.
256 devices in a mesh: row: 16 (over z, core), col: 16 (over x, y).
Axes of the slice: x: 4, y: 4, z: 8, core: 2. Of those that a mesh axis runs over, the one named last changes fastest.
Arguments:
- token_ids: int32 [32, 256], P('row'), may hold values from 0 to 16383
- passage_lengths: int32 [32], P('row'), may hold values from 64 to 256, as said below
- embedding: bfloat16 [16384, 4096], P(None, 'col'), may hold values from -8 to 8
- attn_gain: bfloat16 [4096], P('col'), may hold values from 0.25 to 1.75
- final_gain: bfloat16 [4096], P('col'), may hold values from 0.25 to 1.75
- query_weight: bfloat16 [4096, 4096], P('row', 'col'), may hold values from -0.5 to 0.5
- key_weight: bfloat16 [4096, 4096], P('row', 'col'), may hold values from -0.5 to 0.5
- value_weight: bfloat16 [4096, 4096], P('row', 'col'), may hold values from -0.09375 to 0.09375
- out_weight: bfloat16 [4096, 4096], P('row', 'col'), may hold values from -0.09375 to 0.09375
- crosskey_weight: bfloat16 [4096, 4096], P('row', 'col'), may hold values from -0.09375 to 0.09375
- crossvalue_weight: bfloat16 [4096, 4096], P('row', 'col'), may hold values from -0.09375 to 0.09375
Outputs:
- hidden_out: bfloat16 [8192, 4096], P('row', 'col')
- cross_keys: bfloat16 [8192, 16, 256], P('row', 'col')
- cross_values: bfloat16 [8192, 16, 256], P('row', 'col')
Inputs may be any that keep to these rules, and one draw needn't show every extreme that they name: `passage_lengths`: some passage of every draw has all 256 slots valid.
All inputs are finite; a program needn't handle non-finite values.
Results may differ from a plain program's by a relative error of at most 0.0082.
Values may be sent and summed in bfloat16 or wider, within the bound.
No kernel may reach another device: no remote copies, remote signals or barrier semaphores. Data moves between devices by JAX's collectives and lax.ppermute only.
A program may use at most 64 MiB of HBM per device.

v0:
```python
import jax
import jax.numpy as jnp
from jax import lax
from jax.sharding import PartitionSpec as P

D = 4096
HD = 256
PLEN = 256
epsilon = 1e-06
masked_score = -1000000000.0


def scaled_rows(widened, summed, gain_row):
    inverse = lax.rsqrt(summed / D + epsilon)
    return (widened * inverse * gain_row.astype(jnp.float32)).astype(jnp.bfloat16)


def spread_norm(row_block, gain_row, which):
    widened = row_block.astype(jnp.float32)
    partial_sum = jnp.sum(widened * widened, axis=1, keepdims=True)
    if which == 0:
        summed = lax.psum(partial_sum, "col")
        return lax.all_gather(
            scaled_rows(widened, summed, gain_row[None, :]), "col", axis=1, tiled=True
        )
    else:
        summed = lax.psum(partial_sum, "col")
        return lax.all_gather(
            scaled_rows(widened, summed, gain_row[None, :]), "col", axis=1, tiled=True
        )


def add_terms(source, pieces):
    return tuple(
        (
            jnp.dot(source, weight_piece, preferred_element_type=jnp.float32)
            for weight_piece in pieces
        )
    )


def attend(query_rows, key_rows, value_rows, passage_lengths):
    tok_rows, local_width = query_rows.shape
    passages_here = tok_rows // PLEN
    heads_here = local_width // HD
    query_four = query_rows.reshape(passages_here, PLEN, heads_here, HD)
    key_four = key_rows.reshape(passages_here, PLEN, heads_here, HD)
    value_four = value_rows.reshape(passages_here, PLEN, heads_here, HD)
    scores = jnp.einsum(
        "pihd,pjhd->phij", query_four, key_four, preferred_element_type=jnp.float32
    ) * HD ** (-0.5)
    valid = jnp.arange(PLEN, dtype=jnp.int32)[None, :] < passage_lengths[:, None]
    scores = jnp.where(valid[:, None, None, :], scores, masked_score)
    highest = jnp.max(scores, axis=-1, keepdims=True)
    expon = jnp.exp(scores - highest)
    probs = (expon / jnp.sum(expon, axis=-1, keepdims=True)).astype(jnp.bfloat16)
    mixed = jnp.einsum("phij,pjhd->pihd", probs, value_four, preferred_element_type=jnp.float32)
    return mixed.astype(jnp.bfloat16).reshape(tok_rows, local_width)


def shards(
    token_ids,
    passage_lengths,
    embedding,
    attn_gain,
    final_gain,
    query_weight,
    key_weight,
    value_weight,
    out_weight,
    crosskey_weight,
    crossvalue_weight,
):
    embedded = jnp.take(embedding, token_ids.reshape(-1), axis=0)
    normed = spread_norm(embedded, attn_gain, 0)
    tok_rows = normed.shape[0]
    local_width = query_weight.shape[1]
    query_sum, key_sum, value_sum = add_terms(
        normed,
        (
            lax.all_gather(query_weight, "row", axis=0, tiled=True),
            lax.all_gather(key_weight, "row", axis=0, tiled=True),
            lax.all_gather(value_weight, "row", axis=0, tiled=True),
        ),
    )
    attended = attend(
        query_sum.astype(jnp.bfloat16),
        key_sum.astype(jnp.bfloat16),
        value_sum.astype(jnp.bfloat16),
        passage_lengths,
    )
    heads_full = lax.all_gather(attended, "col", axis=1, tiled=True)
    (projected,) = add_terms(heads_full, (lax.all_gather(out_weight, "row", axis=0, tiled=True),))
    hidden_out = (embedded.astype(jnp.float32) + projected).astype(jnp.bfloat16)
    final_normed = spread_norm(hidden_out, final_gain, 1)
    crosskey_sum, crossvalue_sum = add_terms(
        final_normed,
        (
            lax.all_gather(crosskey_weight, "row", axis=0, tiled=True),
            lax.all_gather(crossvalue_weight, "row", axis=0, tiled=True),
        ),
    )
    heads_here = local_width // HD
    cross_keys = crosskey_sum.astype(jnp.bfloat16).reshape(tok_rows, heads_here, HD)
    cross_values = crossvalue_sum.astype(jnp.bfloat16).reshape(tok_rows, heads_here, HD)
    return (hidden_out, cross_keys, cross_values)


def solution(mesh):
    return jax.shard_map(
        shards,
        mesh=mesh,
        in_specs=(
            P("row", None),
            P("row"),
            P(None, "col"),
            P("col"),
            P("col"),
            P("row", "col"),
            P("row", "col"),
            P("row", "col"),
            P("row", "col"),
            P("row", "col"),
            P("row", "col"),
        ),
        out_specs=(P("row", "col"), P("row", "col", None), P("row", "col", None)),
        check_vma=False,
    )
```

profile of v0, /device:TPU:1, one launch (start us, length us, event | category | flops | bytes accessed | tf_op | source)
XLA Modules:
  0.0 447.0 jit_solution(17359749313425114075)
XLA Ops:
  7.2 0.0 copy-start
  7.2 0.0 all-gather.14.cloned.1.call-start
  7.2 0.7 all-gather.14.cloned.1.call-update
  7.9 0.0 all-gather.10.cloned.1.call-start
  8.0 0.7 convert_element_type.53
  8.6 0.7 copy.22
  9.3 0.0 copy-start.1
  9.3 6.0 %gather_fusion = bf16[512,256]{1,0:T(8,128)(2,1)S(1)} fusion(bf16[16384,256]{1,0:T(8,128)(2,1)} %param.13, s32[1024]{0:T(1024)S(1)} %pad_clamp_fusion), kind=kCustom, calls=%fused_computation | custom fusion | bytes 526336 | tf_op jit(solution)/shard_map/jit(_take)/gather | solution.py:74
  15.4 0.1 copy.17
  15.5 0.0 copy-done
  15.5 0.1 fusion.10
  15.6 34.2 %psum.14 = f32[512,1]{0,1:T(1,128)S(1)} all-reduce(f32[512,1]{0,1:T(1,128)S(1)} %bitcast.48), channel_id=1, replica_groups=mesh['row'=16,'col'=16] {'col'}, use_global_device_ids=true, to_apply=%region_1.2 | all-reduce | flops 512 | bytes 4096 | tf_op jit(solution)/shard_map/psum | solution.py:22
  49.9 0.8 fusion.12
  50.7 0.0 all-gather.10.cloned.1.call-update
  50.7 0.0 all-gather.16.cloned.1.call-start
  50.8 0.7 all-gather.16.cloned.1.call-update
  51.5 0.0 all-gather.12.cloned.1.call-start
  51.5 0.5 all-gather.12.cloned.1.call-update
  52.0 0.0 all-gather.20.cloned.1.call-start
  52.1 0.5 all-gather.20.cloned.1.call-update
  52.6 0.0 all-gather.18.cloned.1.call-start
  52.7 0.0 copy-done.1
  52.7 0.1 iota_compare_fusion
  52.8 0.7 all-gather.14.cloned.1.call-done
  53.5 58.8 %all-gather.10.cloned.1.call-done = bf16[512,4096]{0,1:T(8,128)(2,1)} async-done(((bf16[512,256]{0,1:T(8,128)(2,1)}), bf16[512,4096]{0,1:T(8,128)(2,1)}) %all-gather.10.cloned.1.call-update) | async-done | bytes 4194320 | tf_op jit(solution)/shard_map/all_gather | solution.py:23
  112.3 4.2 convolution_convert_fusion.4
  116.4 37.4 %all-gather.16.cloned.1.call-done = bf16[4096,256]{1,0:T(8,128)(2,1)} async-done(((bf16[256,256]{1,0:T(8,128)(2,1)}), bf16[4096,256]{1,0:T(8,128)(2,1)}) %all-gather.16.cloned.1.call-update) | async-done | bytes 2097168 | tf_op jit(solution)/shard_map/all_gather | solution.py:82
  153.9 4.2 convolution_convert_fusion.3
  158.0 0.4 fusion.15
  158.4 0.3 fusion.3
  158.7 34.7 %all-gather.12.cloned.1.call-done = bf16[4096,256]{1,0:T(8,128)(2,1)} async-done(((bf16[256,256]{1,0:T(8,128)(2,1)}), bf16[4096,256]{1,0:T(8,128)(2,1)}) %all-gather.12.cloned.1.call-update) | async-done | bytes 2097168 | tf_op jit(solution)/shard_map/all_gather | solution.py:83
  193.4 4.2 convolution_convert_fusion.5
  197.6 0.0 copy-start.2
  197.6 1.0 convolution_convert_fusion.2
  198.6 0.0 all-gather.18.cloned.1.call-update
  198.6 0.0 all-gather.24.cloned.1.call-start
  198.7 0.7 all-gather.24.cloned.1.call-update
  199.4 0.0 all-gather.22.cloned.1.call-start
  199.4 0.0 copy-done.2
  199.5 33.5 %all-gather.20.cloned.1.call-done = bf16[4096,256]{1,0:T(8,128)(2,1)} async-done(((bf16[256,256]{1,0:T(8,128)(2,1)}), bf16[4096,256]{1,0:T(8,128)(2,1)}) %all-gather.20.cloned.1.call-update) | async-done | bytes 2097168 | tf_op jit(solution)/shard_map/all_gather | solution.py:93
  232.9 61.3 %all-gather.18.cloned.1.call-done = bf16[512,4096]{1,0:T(8,128)(2,1)} async-done(((bf16[512,256]{1,0:T(8,128)(2,1)}), bf16[512,4096]{1,0:T(8,128)(2,1)}) %all-gather.18.cloned.1.call-update) | async-done | bytes 4194320 | tf_op jit(solution)/shard_map/all_gather | solution.py:92
  294.2 4.2 fusion.7
  298.4 31.3 %psum.15 = f32[512,1]{0,1:T(1,128)S(1)} all-reduce(f32[512,1]{0,1:T(1,128)S(1)} %bitcast.54), channel_id=1, replica_groups=mesh['row'=16,'col'=16] {'col'}, use_global_device_ids=true, to_apply=%region_5.6 | all-reduce | flops 512 | bytes 4096 | tf_op jit(solution)/shard_map/psum | solution.py:27
  329.7 0.8 fusion.9
  330.5 0.0 all-gather.22.cloned.1.call-update
  330.5 0.0 all-gather.26.cloned.1.call-start
  330.6 0.7 all-gather.26.cloned.1.call-update
  331.3 0.8 copy.19
  332.1 4.6 %all-gather.24.cloned.1.call-done = bf16[4096,256]{1,0:T(8,128)(2,1)} async-done(((bf16[256,256]{1,0:T(8,128)(2,1)}), bf16[4096,256]{1,0:T(8,128)(2,1)}) %all-gather.24.cloned.1.call-update) | async-done | bytes 2097168 | tf_op jit(solution)/shard_map/all_gather | solution.py:99
  336.7 57.3 %all-gather.22.cloned.1.call-done = bf16[512,4096]{0,1:T(8,128)(2,1)} async-done(((bf16[512,256]{0,1:T(8,128)(2,1)}), bf16[512,4096]{0,1:T(8,128)(2,1)}) %all-gather.22.cloned.1.call-update) | async-done | bytes 4194320 | tf_op jit(solution)/shard_map/all_gather | solution.py:28
  394.0 4.9 %fusion.5 = bf16[512,1,256]{2,0,1:T(8,128)(2,1)} fusion(bf16[512,4096]{0,1:T(8,128)(2,1)} %all-gather.22.cloned.1.call-done, bf16[4096,256]{1,0:T(8,128)(2,1)} %all-gather.24.cloned.1.call-done), kind=kOutput, calls=%fused_computation.14 | convolution fusion | flops 1073872896 | bytes 6553600 | tf_op jit(solution)/shard_map/dot_general | solution.py:36
  398.8 36.7 %all-gather.26.cloned.1.call-done = bf16[4096,256]{1,0:T(8,128)(2,1)} async-done(((bf16[256,256]{1,0:T(8,128)(2,1)}), bf16[4096,256]{1,0:T(8,128)(2,1)}) %all-gather.26.cloned.1.call-update) | async-done | bytes 2097168 | tf_op jit(solution)/shard_map/all_gather | solution.py:100
  435.6 4.9 %fusion.6 = bf16[512,1,256]{2,0,1:T(8,128)(2,1)} fusion(bf16[512,4096]{0,1:T(8,128)(2,1)} %all-gather.22.cloned.1.call-done, bf16[4096,256]{1,0:T(8,128)(2,1)} %all-gather.26.cloned.1.call-done), kind=kOutput, calls=%fused_computation.15 | convolution fusion | flops 1073872896 | bytes 6553600 | tf_op jit(solution)/shard_map/dot_general | solution.py:36
  (7 shorter events, 0.1 us)
Async XLA Ops:
  7.2 8.3 %copy-start = (s32[2,256]{1,0:T(2,128)S(1)}, s32[2,256]{1,0:T(2,128)}, u32[]{:S(2)}) copy-start(s32[2,256]{1,0:T(2,128)} %param.11) | copy-start | bytes 6148
  7.2 46.3 %all-gather.14.cloned.1.call-start = ((), (), s32[]{:S(2)}) async-start(), calls=%async_computation.2 | async-start | bytes 2228224 | tf_op jit(solution)/shard_map/all_gather | solution.py:81
  7.9 104.3 %all-gather.10.cloned.1.call-start = ((), (), s32[]{:S(2)}) async-start(), calls=%async_computation | async-start | bytes 4456448 | tf_op jit(solution)/shard_map/all_gather | solution.py:23
  9.3 43.4 %copy-start.1 = (s32[2]{0:T(128)S(1)}, s32[2]{0:T(128)}, u32[]{:S(2)}) copy-start(s32[2]{0:T(128)} %param.12) | copy-start | bytes 28
  50.7 103.1 %all-gather.16.cloned.1.call-start = ((), (), s32[]{:S(2)}) async-start(), calls=%async_computation.3 | async-start | bytes 2228224 | tf_op jit(solution)/shard_map/all_gather | solution.py:82
  51.5 141.9 %all-gather.12.cloned.1.call-start = ((), (), s32[]{:S(2)}) async-start(), calls=%async_computation.1 | async-start | bytes 2228224 | tf_op jit(solution)/shard_map/all_gather | solution.py:83
  52.0 180.9 %all-gather.20.cloned.1.call-start = ((), (), s32[]{:S(2)}) async-start(), calls=%async_computation.5 | async-start | bytes 2228224 | tf_op jit(solution)/shard_map/all_gather | solution.py:93
  52.6 241.6 %all-gather.18.cloned.1.call-start = ((), (), s32[]{:S(2)}) async-start(), calls=%async_computation.4 | async-start | bytes 4456448 | tf_op jit(solution)/shard_map/all_gather | solution.py:92
  197.6 1.9 copy-start.2
  198.6 138.1 %all-gather.24.cloned.1.call-start = ((), (), s32[]{:S(2)}) async-start(), calls=%async_computation.7 | async-start | bytes 2228224 | tf_op jit(solution)/shard_map/all_gather | solution.py:99
  199.4 194.6 %all-gather.22.cloned.1.call-start = ((), (), s32[]{:S(2)}) async-start(), calls=%async_computation.6 | async-start | bytes 4456448 | tf_op jit(solution)/shard_map/all_gather | solution.py:28
  330.5 105.1 %all-gather.26.cloned.1.call-start = ((), (), s32[]{:S(2)}) async-start(), calls=%async_computation.8 | async-start | bytes 2228224 | tf_op jit(solution)/shard_map/all_gather | solution.py:100
Sparse Core Ops, SparseCore 0:
  9.8 43.6 all-gather.13
  56.5 55.7 all-gather.9
  114.1 39.7 all-gather.15
  155.5 37.8 all-gather.11
  195.1 37.8 all-gather.19
  235.7 58.4 all-gather.17
  296.0 40.6 all-gather.23
  339.7 54.2 all-gather.21
  395.8 39.7 all-gather.25
where the time goes:
time: 447 us
  waiting for transfers between devices  329 us (74%)
  blocking collectives  65.5 us (15%)
  matrix products  28.1 us (6%)
  between operations  14 us (3%)
  local copies, waits for them, and re-layouts  7.71 us (2%)
    all_gather x2, waiting for transfers between devices, spread_norm(): lax.all_gather(scaled_rows(widened, summed, gain_row[None, :]), 'col', ax...  116 us
    psum x2, blocking collectives, spread_norm(): summed = lax.psum(partial_sum, 'col')  65.5 us
    all_gather x1, waiting for transfers between devices, shards(): heads_full = lax.all_gather(attended, 'col', axis=1, tiled=True)  61.3 us
    all_gather x1, waiting for transfers between devices, shards(): lax.all_gather(key_weight, 'row', axis=0, tiled=True)  37.4 us
    all_gather x1, waiting for transfers between devices, shards(): lax.all_gather(crossvalue_weight, 'row', axis=0, tiled=True)  36.7 us
    all_gather x1, waiting for transfers between devices, shards(): lax.all_gather(value_weight, 'row', axis=0, tiled=True)  34.7 us
    all_gather x1, waiting for transfers between devices, shards(): lax.all_gather(out_weight, 'row', axis=0, tiled=True)  33.5 us
    dot_general x6, matrix products, add_terms(): jnp.dot(source, weight_piece, preferred_element_type=jnp.float32)  26.4 us
  transfers between devices with their start and end apart: 9, of which 9 were waited for; matrix products, arithmetic and copies ran while one was open for 7% of the time, Pallas kernels for 0%

commit v1 on v0

--- a/solution.py
+++ b/solution.py
@@ -2,6 +2,7 @@
 import jax.numpy as jnp
 from jax import lax
 from jax.sharding import PartitionSpec as P
+from jax.lax import all_gather
 
 D = 4096
 HD = 256
@@ -19,7 +20,7 @@
     widened = row_block.astype(jnp.float32)
     partial_sum = jnp.sum(widened * widened, axis=1, keepdims=True)
     if which == 0:
-        summed = lax.psum(partial_sum, "col")
+        summed = jnp.sum(all_gather(partial_sum, "col"), axis=0)
         return lax.all_gather(
             scaled_rows(widened, summed, gain_row[None, :]), "col", axis=1, tiled=True
         )

time: 447 us -> 446 us (level)
  blocking collectives: 65.5 us -> 51.1 us
  waiting for transfers between devices: 329 us -> 342 us
    psum x2 -> x1, blocking collectives: 65.5 us -> 31.3 us  [spread_norm(): summed = lax.psum(partial_sum, 'col')]
    all_gather x0 -> x1, blocking collectives: none -> 19.8 us  [spread_norm(): summed = jnp.sum(all_gather(partial_sum, 'col'), axis=0)]
    all_gather x1, waiting for transfers between devices: 0.71 us -> 15.1 us  [shards(): lax.all_gather(query_weight, 'row', axis=0, tiled=True)]
  transfers between devices with their start and end apart: 9 -> 9, of which waited for: 9 -> 9; matrix products, arithmetic and copies ran while one was open for 7% -> 8% of each run, Pallas kernels for 0% -> 0%
where the time goes in v1:
time: 446 us; the launch traced here: 445 us
  waiting for transfers between devices  342 us (77%)
  blocking collectives  51.1 us (11%)
  matrix products  28.1 us (6%)
  between operations  14 us (3%)
  local copies, waits for them, and re-layouts  7.71 us (2%)
    all_gather x2, waiting for transfers between devices, spread_norm(): lax.all_gather(scaled_rows(widened, summed, gain_row[None, :]), 'col', ax...  115 us
    all_gather x1, waiting for transfers between devices, shards(): heads_full = lax.all_gather(attended, 'col', axis=1, tiled=True)  61.3 us
    all_gather x1, waiting for transfers between devices, shards(): lax.all_gather(key_weight, 'row', axis=0, tiled=True)  37.4 us
    all_gather x1, waiting for transfers between devices, shards(): lax.all_gather(crossvalue_weight, 'row', axis=0, tiled=True)  36.7 us
    all_gather x1, waiting for transfers between devices, shards(): lax.all_gather(value_weight, 'row', axis=0, tiled=True)  34.7 us
    all_gather x1, waiting for transfers between devices, shards(): lax.all_gather(out_weight, 'row', axis=0, tiled=True)  33.5 us
    psum x1, blocking collectives, spread_norm(): summed = lax.psum(partial_sum, 'col')  31.3 us
    dot_general x6, matrix products, add_terms(): jnp.dot(source, weight_piece, preferred_element_type=jnp.float32)  26.4 us
  transfers between devices with their start and end apart: 9, of which 9 were waited for; matrix products, arithmetic and copies ran while one was open for 8% of the time, Pallas kernels for 0%

profile of v1, /device:TPU:1, one launch (start us, length us, event | category | flops | bytes accessed | tf_op | source)
XLA Modules:
  0.0 445.5 jit_solution(10929252409085733325)
XLA Ops:
  7.2 0.0 copy-start
  7.2 0.0 all-gather.16.cloned.1.call-start
  7.2 0.7 all-gather.16.cloned.1.call-update
  7.9 0.0 all-gather.12.cloned.1.call-start
  8.0 0.7 convert_element_type.53
  8.6 0.7 copy.25
  9.3 0.0 copy-start.1
  9.3 6.0 %gather_fusion = bf16[512,256]{1,0:T(8,128)(2,1)S(1)} fusion(bf16[16384,256]{1,0:T(8,128)(2,1)} %param.13, s32[1024]{0:T(1024)S(1)} %pad_clamp_fusion), kind=kCustom, calls=%fused_computation | custom fusion | bytes 526336 | tf_op jit(solution)/shard_map/jit(_take)/gather | solution.py:75
  15.4 0.1 copy.20
  15.5 0.0 copy-done
  15.5 0.1 fusion.10
  15.6 19.8 %all-gather.1 = f32[16,1,512]{2,1,0:T(1,128)S(1)} all-gather(f32[1,1,512]{2,1,0:T(1,128)S(1)} %bitcast.45), channel_id=2, replica_groups=mesh['row'=16,'col'=16] {'col'}, dimensions={0}, use_global_device_ids=true | all-gather | bytes 34816 | tf_op jit(solution)/shard_map/all_gather | solution.py:23
  35.5 0.8 fusion.12
  36.3 0.0 all-gather.12.cloned.1.call-update
  36.3 0.0 all-gather.18.cloned.1.call-start
  36.4 0.7 all-gather.18.cloned.1.call-update
  37.1 0.0 all-gather.14.cloned.1.call-start
  37.1 0.5 all-gather.14.cloned.1.call-update
  37.6 0.0 all-gather.22.cloned.1.call-start
  37.7 0.5 all-gather.22.cloned.1.call-update
  38.2 0.0 all-gather.20.cloned.1.call-start
  38.3 0.0 copy-done.1
  38.3 0.1 iota_compare_fusion
  38.4 15.1 %all-gather.16.cloned.1.call-done = bf16[4096,256]{1,0:T(8,128)(2,1)} async-done(((bf16[256,256]{1,0:T(8,128)(2,1)}), bf16[4096,256]{1,0:T(8,128)(2,1)}) %all-gather.16.cloned.1.call-update) | async-done | bytes 2097168 | tf_op jit(solution)/shard_map/all_gather | solution.py:82
  53.5 57.3 %all-gather.12.cloned.1.call-done = bf16[512,4096]{0,1:T(8,128)(2,1)} async-done(((bf16[512,256]{0,1:T(8,128)(2,1)}), bf16[512,4096]{0,1:T(8,128)(2,1)}) %all-gather.12.cloned.1.call-update) | async-done | bytes 4194320 | tf_op jit(solution)/shard_map/all_gather | solution.py:24
  110.7 4.2 convolution_convert_fusion.4
  114.9 37.4 %all-gather.18.cloned.1.call-done = bf16[4096,256]{1,0:T(8,128)(2,1)} async-done(((bf16[256,256]{1,0:T(8,128)(2,1)}), bf16[4096,256]{1,0:T(8,128)(2,1)}) %all-gather.18.cloned.1.call-update) | async-done | bytes 2097168 | tf_op jit(solution)/shard_map/all_gather | solution.py:83
  152.4 4.2 convolution_convert_fusion.3
  156.5 0.4 fusion.15
  156.9 0.3 fusion.3
  157.2 34.7 %all-gather.14.cloned.1.call-done = bf16[4096,256]{1,0:T(8,128)(2,1)} async-done(((bf16[256,256]{1,0:T(8,128)(2,1)}), bf16[4096,256]{1,0:T(8,128)(2,1)}) %all-gather.14.cloned.1.call-update) | async-done | bytes 2097168 | tf_op jit(solution)/shard_map/all_gather | solution.py:84
  191.9 4.2 convolution_convert_fusion.5
  196.1 0.0 copy-start.2
  196.1 1.0 convolution_convert_fusion.2
  197.1 0.0 all-gather.20.cloned.1.call-update
  197.1 0.0 all-gather.26.cloned.1.call-start
  197.2 0.7 all-gather.26.cloned.1.call-update
  197.9 0.0 all-gather.24.cloned.1.call-start
  197.9 0.0 copy-done.2
  197.9 33.5 %all-gather.22.cloned.1.call-done = bf16[4096,256]{1,0:T(8,128)(2,1)} async-done(((bf16[256,256]{1,0:T(8,128)(2,1)}), bf16[4096,256]{1,0:T(8,128)(2,1)}) %all-gather.22.cloned.1.call-update) | async-done | bytes 2097168 | tf_op jit(solution)/shard_map/all_gather | solution.py:94
  231.4 61.3 %all-gather.20.cloned.1.call-done = bf16[512,4096]{1,0:T(8,128)(2,1)} async-done(((bf16[512,256]{1,0:T(8,128)(2,1)}), bf16[512,4096]{1,0:T(8,128)(2,1)}) %all-gather.20.cloned.1.call-update) | async-done | bytes 4194320 | tf_op jit(solution)/shard_map/all_gather | solution.py:93
  292.7 4.2 fusion.7
  296.9 31.3 %psum.7 = f32[512,1]{0,1:T(1,128)S(1)} all-reduce(f32[512,1]{0,1:T(1,128)S(1)} %bitcast.52), channel_id=1, replica_groups=mesh['row'=16,'col'=16] {'col'}, use_global_device_ids=true, to_apply=%region_5.6 | all-reduce | flops 512 | bytes 4096 | tf_op jit(solution)/shard_map/psum | solution.py:28
  328.2 0.8 fusion.9
  329.0 0.0 all-gather.24.cloned.1.call-update
  329.0 0.0 all-gather.28.cloned.1.call-start
  329.1 0.7 all-gather.28.cloned.1.call-update
  329.8 0.8 copy.22
  330.6 4.6 %all-gather.26.cloned.1.call-done = bf16[4096,256]{1,0:T(8,128)(2,1)} async-done(((bf16[256,256]{1,0:T(8,128)(2,1)}), bf16[4096,256]{1,0:T(8,128)(2,1)}) %all-gather.26.cloned.1.call-update) | async-done | bytes 2097168 | tf_op jit(solution)/shard_map/all_gather | solution.py:100
  335.2 57.3 %all-gather.24.cloned.1.call-done = bf16[512,4096]{0,1:T(8,128)(2,1)} async-done(((bf16[512,256]{0,1:T(8,128)(2,1)}), bf16[512,4096]{0,1:T(8,128)(2,1)}) %all-gather.24.cloned.1.call-update) | async-done | bytes 4194320 | tf_op jit(solution)/shard_map/all_gather | solution.py:29
  392.5 4.9 %fusion.5 = bf16[512,1,256]{2,0,1:T(8,128)(2,1)} fusion(bf16[512,4096]{0,1:T(8,128)(2,1)} %all-gather.24.cloned.1.call-done, bf16[4096,256]{1,0:T(8,128)(2,1)} %all-gather.26.cloned.1.call-done), kind=kOutput, calls=%fused_computation.14 | convolution fusion | flops 1073872896 | bytes 6553600 | tf_op jit(solution)/shard_map/dot_general | solution.py:37
  397.3 36.7 %all-gather.28.cloned.1.call-done = bf16[4096,256]{1,0:T(8,128)(2,1)} async-done(((bf16[256,256]{1,0:T(8,128)(2,1)}), bf16[4096,256]{1,0:T(8,128)(2,1)}) %all-gather.28.cloned.1.call-update) | async-done | bytes 2097168 | tf_op jit(solution)/shard_map/all_gather | solution.py:101
  434.1 4.9 %fusion.6 = bf16[512,1,256]{2,0,1:T(8,128)(2,1)} fusion(bf16[512,4096]{0,1:T(8,128)(2,1)} %all-gather.24.cloned.1.call-done, bf16[4096,256]{1,0:T(8,128)(2,1)} %all-gather.28.cloned.1.call-done), kind=kOutput, calls=%fused_computation.15 | convolution fusion | flops 1073872896 | bytes 6553600 | tf_op jit(solution)/shard_map/dot_general | solution.py:37
  (8 shorter events, 0.1 us)
Async XLA Ops:
  7.2 8.3 %copy-start = (s32[2,256]{1,0:T(2,128)S(1)}, s32[2,256]{1,0:T(2,128)}, u32[]{:S(2)}) copy-start(s32[2,256]{1,0:T(2,128)} %param.11) | copy-start | bytes 6148
  7.2 46.3 %all-gather.16.cloned.1.call-start = ((), (), s32[]{:S(2)}) async-start(), calls=%async_computation.2 | async-start | bytes 2228224 | tf_op jit(solution)/shard_map/all_gather | solution.py:82
  7.9 102.8 %all-gather.12.cloned.1.call-start = ((), (), s32[]{:S(2)}) async-start(), calls=%async_computation | async-start | bytes 4456448 | tf_op jit(solution)/shard_map/all_gather | solution.py:24
  9.3 29.0 %copy-start.1 = (s32[2]{0:T(128)S(1)}, s32[2]{0:T(128)}, u32[]{:S(2)}) copy-start(s32[2]{0:T(128)} %param.12) | copy-start | bytes 28
  36.3 116.0 %all-gather.18.cloned.1.call-start = ((), (), s32[]{:S(2)}) async-start(), calls=%async_computation.3 | async-start | bytes 2228224 | tf_op jit(solution)/shard_map/all_gather | solution.py:83
  37.1 154.8 %all-gather.14.cloned.1.call-start = ((), (), s32[]{:S(2)}) async-start(), calls=%async_computation.1 | async-start | bytes 2228224 | tf_op jit(solution)/shard_map/all_gather | solution.py:84
  37.6 193.8 %all-gather.22.cloned.1.call-start = ((), (), s32[]{:S(2)}) async-start(), calls=%async_computation.5 | async-start | bytes 2228224 | tf_op jit(solution)/shard_map/all_gather | solution.py:94
  38.2 254.5 %all-gather.20.cloned.1.call-start = ((), (), s32[]{:S(2)}) async-start(), calls=%async_computation.4 | async-start | bytes 4456448 | tf_op jit(solution)/shard_map/all_gather | solution.py:93
  196.1 1.9 copy-start.2
  197.1 138.1 %all-gather.26.cloned.1.call-start = ((), (), s32[]{:S(2)}) async-start(), calls=%async_computation.7 | async-start | bytes 2228224 | tf_op jit(solution)/shard_map/all_gather | solution.py:100
  197.9 194.6 %all-gather.24.cloned.1.call-start = ((), (), s32[]{:S(2)}) async-start(), calls=%async_computation.6 | async-start | bytes 4456448 | tf_op jit(solution)/shard_map/all_gather | solution.py:29
  329.0 105.1 %all-gather.28.cloned.1.call-start = ((), (), s32[]{:S(2)}) async-start(), calls=%async_computation.8 | async-start | bytes 2228224 | tf_op jit(solution)/shard_map/all_gather | solution.py:101
Sparse Core Ops, SparseCore 0:
  9.8 43.6 all-gather.15
  56.5 54.2 all-gather.11
  112.6 39.7 all-gather.17
  154.0 37.8 all-gather.13
  193.6 37.8 all-gather.21
  234.2 58.4 all-gather.19
  294.5 40.6 all-gather.25
  338.2 54.2 all-gather.23
  394.3 39.7 all-gather.27
